TPU v7x, 128 devices: a whole 4x4x4 slice. The times are simulated.
128 devices in a mesh: col: 32 (over x, z, core), leg: 4 (over y).
Axes of the slice: x: 4, y: 4, z: 4, core: 2. Of those that a mesh axis runs over, the one named last changes fastest.
Arguments:
- coeffs: float32 [2048, 4, 128, 128], P(('col', 'leg')), may hold values from -0.5 to 0.5
- block_ids: int32 [2048, 4], P(('col', 'leg')), may hold values from 0 to 127
- col_counts: int32 [2048], P(('col', 'leg')), may hold values from 1 to 128
- primal: float32 [2048, 128], P(('col', 'leg')), may hold values from 0.3 to 3
- slack: float32 [2048, 128], P(('col', 'leg')), may hold values from 0.3 to 3
- cost: float32 [2048, 128], P(('col', 'leg')), may hold values from -6 to 6
- duals: float32 [128, 128], P('leg'), may hold values from -6 to 6
- demand: float32 [128, 128], P('leg'), may hold values from -6 to 6
Outputs:
- step_dual: float32 [128, 128], P('leg')
- step_primal: float32 [2048, 128], P(('col', 'leg'))
Inputs may be any that keep to these rules, and one draw needn't show every extreme that they name: `block_ids`: leg block of each tile; many tiles may share a block, the tiles of one column group too. `col_counts`: columns at or after this count in a column group are padding.
All inputs are finite; a program needn't handle non-finite values.
Results may differ from a plain program's by a relative error of at most 0.0003.
Values sent between devices are 32-bit elements; how exact they have to be, the bound alone decides.
No kernel may reach another device: no remote copies, remote signals or barrier semaphores. Data moves between devices by JAX's collectives and lax.ppermute only.
A program may use at most 128 MiB of HBM per device.

v0:
```python
import jax
import jax.numpy as jnp
from jax import lax
from jax.sharding import PartitionSpec as P

ITERS = 3
SIGMA = 0.3
REGULAR = 1.0
PRECISE = lax.Precision.HIGHEST


def invert_blocks(blocks):
    identity = jnp.eye(blocks.shape[1], dtype=jnp.float32)

    def invert_one(matrix):
        factor = jnp.linalg.cholesky(matrix)
        return jax.scipy.linalg.cho_solve((factor, True), identity)

    return jax.vmap(invert_one)(blocks + REGULAR * identity)


def per_device(coeffs, block_ids, col_counts, primal, slack, cost, duals, demand):
    lb_dev = duals.shape[0]
    group_count = coeffs.shape[0]
    span = coeffs.shape[1]
    rows_tile = coeffs.shape[2]
    columns = coeffs.shape[3]
    tile_count = group_count * span
    leg_count = lax.axis_size("leg")
    total_blocks = lb_dev * leg_count
    valid = (jnp.arange(columns, dtype=jnp.int32)[None, :] < col_counts[:, None]).astype(
        jnp.float32
    )
    tile_vals = coeffs * valid[:, None, None, :]
    totals_pair = lax.psum((jnp.sum(valid * primal * slack), jnp.sum(valid)), ("col", "leg"))
    mean_comp = totals_pair[0] / totals_pair[1]
    scaling = primal / slack
    flat_ids = block_ids.reshape(tile_count)
    all_duals = lax.all_gather(duals, "leg", axis=0, tiled=True)
    natural_hot = (flat_ids[:, None] == jnp.arange(total_blocks, dtype=jnp.int32)[None, :]).astype(
        jnp.float32
    )
    dual_tiles = jnp.dot(natural_hot, all_duals, precision=PRECISE).reshape(
        group_count, span, rows_tile
    )
    dual_res = cost - jnp.einsum("gsij,gsi->gj", tile_vals, dual_tiles, precision=PRECISE) - slack
    comp_res = SIGMA * mean_comp - primal * slack
    shifted = primal - scaling * dual_res + comp_res / slack

    def widen_all(vector):
        return lax.all_gather(vector, "leg", axis=0, tiled=True)

    def inner_sum(left, right):
        return lax.psum(jnp.sum(left * right), "leg")

    onehot = (flat_ids[:, None] == jnp.arange(total_blocks, dtype=jnp.int32)[None, :]).astype(
        jnp.float32
    )

    def transpose_apply(whole):
        per_tile = jnp.dot(onehot, whole, precision=PRECISE).reshape(group_count, span, rows_tile)
        return jnp.einsum("gsij,gsi->gj", tile_vals, per_tile, precision=PRECISE)

    def forward_partial(colvec):
        per_tile = jnp.einsum("gsij,gj->gsi", tile_vals, colvec, precision=PRECISE)
        return jnp.dot(onehot.T, per_tile.reshape(tile_count, rows_tile), precision=PRECISE)

    rhs_part = -forward_partial(shifted)
    weighted = tile_vals * scaling[:, None, None, :]
    gram = jnp.einsum("gsij,gskj->gsik", weighted, tile_vals, precision=PRECISE)
    gram = gram.reshape(tile_count, rows_tile, rows_tile)
    block_part = jnp.einsum("tb,tik->bik", onehot, gram, precision=PRECISE)
    rhs_sum, block_sum = lax.psum(
        (
            lax.psum_scatter(rhs_part, "leg", scatter_dimension=0, tiled=True),
            lax.psum_scatter(block_part, "leg", scatter_dimension=0, tiled=True),
        ),
        "col",
    )
    rhs = demand + rhs_sum
    inverse = invert_blocks(block_sum)

    def precondition(vector):
        return jnp.einsum("bij,bj->bi", inverse, vector, precision=PRECISE)

    step_dual = jnp.zeros_like(rhs)
    residual = rhs
    smoothed = precondition(residual)
    direction = smoothed
    norm_now = inner_sum(residual, smoothed)
    for turn in range(ITERS):
        operate_whole = widen_all(direction)
        narrow_shares = lax.psum_scatter(
            forward_partial(scaling * transpose_apply(operate_whole)),
            "leg",
            scatter_dimension=0,
            tiled=True,
        )
        image = lax.psum(narrow_shares, "col") + REGULAR * direction
        step_len = norm_now / inner_sum(direction, image)
        step_dual = step_dual + step_len * direction
        residual = residual - step_len * image
        if turn + 1 < ITERS:
            smoothed = precondition(residual)
            norm_next = inner_sum(residual, smoothed)
            direction = smoothed + norm_next / norm_now * direction
            norm_now = norm_next
    whole_step = widen_all(step_dual)
    step_primal = valid * (
        scaling * transpose_apply(whole_step) + comp_res / slack - scaling * dual_res
    )
    return (
        lax.dynamic_slice_in_dim(whole_step, lax.axis_index("leg") * lb_dev, lb_dev, 0),
        step_primal,
    )


def solution(mesh):
    return jax.shard_map(
        per_device,
        mesh=mesh,
        in_specs=(
            P(("col", "leg"), None, None, None),
            P(("col", "leg"), None),
            P(("col", "leg")),
            P(("col", "leg"), None),
            P(("col", "leg"), None),
            P(("col", "leg"), None),
            P("leg", None),
            P("leg", None),
        ),
        out_specs=(P("leg", None), P(("col", "leg"), None)),
        check_vma=False,
    )
```

profile of v0, /device:TPU:0, one launch (start us, length us, event | category | flops | bytes accessed | tf_op | source)
XLA Modules:
  0.0 1638.2 jit_solution(10132136737136496447)
XLA Ops:
  7.2 0.8 copy.20
  8.1 12.7 all_gather.15
  20.8 0.7 fusion.42
  21.5 0.2 fusion.28
  21.7 1.4 fusion.43
  23.1 66.0 %all-reduce = (f32[]{:T(128)}, f32[]{:T(128)}) all-reduce(f32[]{:T(128)} %get-tuple-element.5, f32[]{:T(128)} %get-tuple-element.4), channel_id=1, replica_groups=mesh['col'=32,'leg'=4] {'col','leg'}, use_global_device_ids=true, to_apply=%region_1.0 | all-reduce | flops 2 | bytes 16 | tf_op jit(solution)/shard_map/psum | solution.py:35
  90.5 4.3 fusion.18
  94.9 8.9 fusion
  103.8 9.5 fusion.2
  113.3 9.3 copy.22
  122.7 5.9 fusion.17
  128.6 1.0 convolution_negate_fusion
  129.6 71.0 %reduce-scatter.8.cloned.1.call-done = f32[32,128,128]{1,2,0:T(8,128)} async-done(((f32[128,128,128]{1,2,0:T(8,128)}), f32[32,128,128]{1,2,0:T(8,128)}) %reduce-scatter.8.cloned.1.call-update) | async-done | bytes 2097168 | tf_op jit(solution)/shard_map/reduce_scatter | solution.py:76
  200.8 22.1 %reduce-scatter.6.cloned.1.call-done = f32[32,128]{1,0:T(8,128)} async-done(((f32[128,128]{1,0:T(8,128)}), f32[32,128]{1,0:T(8,128)}) %reduce-scatter.6.cloned.1.call-update) | async-done | bytes 16400 | tf_op jit(solution)/shard_map/reduce_scatter | solution.py:75
  223.0 126.4 %psum.93 = f32[32,128]{1,0:T(8,128)S(1)} all-reduce(f32[32,128]{1,0:T(8,128)} %reduce-scatter.6.cloned.1.call-done), channel_id=1, replica_groups=mesh['col'=32,'leg'=4] {'col'}, use_global_device_ids=true, to_apply=%region_5.0 | all-reduce | flops 4096 | bytes 32768 | tf_op jit(solution)/shard_map/psum | solution.py:73
  349.4 3.3 broadcast_add_fusion
  352.7 2.9 copy.24
  355.6 3.2 fusion.8
  358.9 375.8 %custom-call.11 = f32[32,128,128]{2,1,0:T(8,128)S(1)} custom-call(f32[32,128,128]{2,1,0:T(8,128)} %fusion.8), custom_call_target="Cholesky" | custom-call | tf_op jit(solution)/shard_map/vmap(jit(cholesky))/cholesky | solution.py:16
  734.6 0.2 select_reduce_fusion
  734.9 1.7 select_bitcast_fusion
  736.6 315.3 %custom-call.12 = f32[32,1,128,128]{2,3,1,0:T(8,128)S(1)} custom-call(f32[32,1,128,128]{3,2,1,0:T(8,128)} %select_bitcast_fusion), custom_call_target="InvertDiagBlocksLowerTriangular" | custom-call | tf_op jit(solution)/shard_map/vmap(jit(_cho_solve))/triangular_solve | solution.py:17
  1051.9 1.3 copy-done.5
  1053.2 3.5 fusion.6
  1056.8 4.0 fusion.4
  1060.7 3.3 fusion.44
  1064.1 12.3 all_gather.16
  1076.4 0.2 fusion.26
  1076.6 2.5 fusion.15
  1079.1 3.7 fusion.14
  1082.8 1.0 fusion.25
  1083.8 15.1 reduce-scatter.10.cloned.1.call-done
  1099.0 126.0 %psum.96 = f32[32,128]{1,0:T(8,128)S(1)} all-reduce(f32[32,128]{1,0:T(8,128)} %reduce-scatter.10.cloned.1.call-done), channel_id=1, replica_groups=mesh['col'=32,'leg'=4] {'col'}, use_global_device_ids=true, to_apply=%region_13.14 | all-reduce | flops 4096 | bytes 32768 | tf_op jit(solution)/shard_map/psum | solution.py:99
  1225.0 0.6 multiply_reduce_fusion.3
  1225.6 9.7 all-reduce.1
  1236.6 3.3 fusion.45
  1240.0 0.6 multiply_reduce_fusion.2
  1240.6 9.0 psum.98
  1250.9 12.2 all_gather.17
  1263.1 0.2 fusion.24
  1263.3 4.2 fusion.13
  1267.5 3.7 fusion.12
  1271.3 1.0 fusion.23
  1272.3 15.1 reduce-scatter.12.cloned.1.call-done
  1287.4 126.0 %psum.99 = f32[32,128]{1,0:T(8,128)S(1)} all-reduce(f32[32,128]{1,0:T(8,128)} %reduce-scatter.12.cloned.1.call-done), channel_id=1, replica_groups=mesh['col'=32,'leg'=4] {'col'}, use_global_device_ids=true, to_apply=%region_19.20 | all-reduce | flops 4096 | bytes 32768 | tf_op jit(solution)/shard_map/psum | solution.py:99
  1413.4 0.6 multiply_reduce_fusion.1
  1414.0 9.7 psum.100
  1425.1 3.3 fusion.46
  1428.4 0.6 multiply_reduce_fusion
  1429.1 9.0 psum.101
  1439.4 12.2 all_gather.18
  1451.6 0.2 fusion.22
  1451.8 4.2 fusion.11
  1456.0 3.7 fusion.10
  1459.8 1.0 fusion.21
  1460.7 15.2 reduce-scatter.14.cloned.1.call-done
  1475.9 126.0 %psum.102 = f32[32,128]{1,0:T(8,128)S(1)} all-reduce(f32[32,128]{1,0:T(8,128)} %reduce-scatter.14.cloned.1.call-done), channel_id=1, replica_groups=mesh['col'=32,'leg'=4] {'col'}, use_global_device_ids=true, to_apply=%region_25.26 | all-reduce | flops 4096 | bytes 32768 | tf_op jit(solution)/shard_map/psum | solution.py:99
  1601.9 0.6 fusion.31
  1602.5 9.7 psum.103
  1613.6 11.9 all_gather.19
  1625.4 0.2 fusion.20
  1625.7 4.2 fusion.16
  1629.9 0.7 subtract_select_fusion
  1630.5 0.6 constant_dynamic-slice_fusion
  (50 shorter events, 0.8 us)
Async XLA Ops:
  7.2 87.7 %copy-start.6 = (f32[16,128]{1,0:T(8,128)S(1)}, f32[16,128]{1,0:T(8,128)}, u32[]{:S(2)}) copy-start(f32[16,128]{1,0:T(8,128)} %param.11) | copy-start | bytes 24580
  7.2 87.7 %copy-start.7 = (f32[16,128]{1,0:T(8,128)S(1)}, f32[16,128]{1,0:T(8,128)}, u32[]{:S(2)}) copy-start(f32[16,128]{1,0:T(8,128)} %param.12) | copy-start | bytes 24580
  7.2 87.7 %copy-start.8 = (f32[16,128]{1,0:T(8,128)S(1)}, f32[16,128]{1,0:T(8,128)}, u32[]{:S(2)}) copy-start(f32[16,128]{1,0:T(8,128)} %param.13) | copy-start | bytes 24580
  7.2 193.4 %reduce-scatter.8.cloned.1.call-start = ((), (), s32[]{:S(2)}) async-start(), calls=%async_computation.6 | async-start | bytes 10485760 | tf_op jit(solution)/shard_map/reduce_scatter | solution.py:76
  90.5 4.4 copy-start
  122.6 226.7 %copy-start.9 = (f32[32,128]{1,0:T(8,128)S(1)}, f32[32,128]{1,0:T(8,128)}, u32[]{:S(2)}) copy-start(f32[32,128]{1,0:T(8,128)} %param.15) | copy-start | bytes 49156
  122.7 100.3 %reduce-scatter.6.cloned.1.call-start = ((), (), s32[]{:S(2)}) async-start(), calls=%async_computation.5 | async-start | bytes 81920 | tf_op jit(solution)/shard_map/reduce_scatter | solution.py:75
  129.6 219.8 %all-reduce.4.cloned.1.call-start = ((), (), s32[]{:S(2)}) async-start(), calls=%async_computation.7 | async-start | bytes 4194304 | tf_op jit(solution)/shard_map/psum | solution.py:73
  200.6 898.3 %reduce-scatter.10.cloned.1.call-start = ((), (), s32[]{:S(2)}) async-start(), calls=%async_computation.8 | async-start | bytes 81920 | tf_op jit(solution)/shard_map/reduce_scatter | solution.py:93
  349.4 6.2 copy-start.4
  1051.9 1.4 copy-start.5
  1056.7 19.9 %copy-start.1 = (f32[16,4,128,128]{3,2,1,0:T(8,128)S(1)}, f32[16,4,128,128]{3,2,1,0:T(8,128)}, u32[]{:S(2)}) copy-start(f32[16,4,128,128]{3,2,1,0:T(8,128)} %param.8) | copy-start | bytes 12582916
  1083.8 203.6 %reduce-scatter.12.cloned.1.call-start = ((), (), s32[]{:S(2)}) async-start(), calls=%async_computation.9 | async-start | bytes 81920 | tf_op jit(solution)/shard_map/reduce_scatter | solution.py:93
  1250.9 16.6 %copy-start.2 = (f32[16,4,128,128]{3,2,1,0:T(8,128)S(1)}, f32[16,4,128,128]{3,2,1,0:T(8,128)}, u32[]{:S(2)}) copy-start(f32[16,4,128,128]{3,2,1,0:T(8,128)} %param.8) | copy-start | bytes 12582916
  1272.2 203.7 %reduce-scatter.14.cloned.1.call-start = ((), (), s32[]{:S(2)}) async-start(), calls=%async_computation.10 | async-start | bytes 81920 | tf_op jit(solution)/shard_map/reduce_scatter | solution.py:93
  1439.4 16.7 %copy-start.3 = (f32[16,4,128,128]{3,2,1,0:T(8,128)S(1)}, f32[16,4,128,128]{3,2,1,0:T(8,128)}, u32[]{:S(2)}) copy-start(f32[16,4,128,128]{3,2,1,0:T(8,128)} %param.8) | copy-start | bytes 12582916
  1456.0 173.8 %copy-start.10 = (s32[16]{0:T(128)S(1)}, s32[16]{0:T(128)}, u32[]{:S(2)}) copy-start(s32[16]{0:T(128)} %param.10) | copy-start | bytes 196
Sparse Core Ops, SparseCore 0:
  122.8 77.7 reduce-scatter.7
  202.9 19.9 reduce-scatter.5
  226.6 107.2 all-reduce.3
  1083.9 15.0 reduce-scatter.9
  1272.4 14.9 reduce-scatter.11
  1460.9 15.0 reduce-scatter.13
where the time goes:
time: 1650 us; the launch traced here: 1640 us
  other arithmetic  706 us (43%)
  blocking collectives  679 us (41%)
  waiting for transfers between devices  139 us (8%)
  matrix products  77.1 us (5%)
  between operations  22.8 us (1%)
    psum x3, blocking collectives, per_device(): image = lax.psum(narrow_shares, 'col') + REGULAR * direction  378 us
    another operation x4, other arithmetic, invert_one(): factor = jnp.linalg.cholesky(matrix)  376 us
    another operation x3, other arithmetic, invert_one(): return jax.scipy.linalg.cho_solve((factor, True), identity)  317 us
    psum x1, blocking collectives, per_device(): lax.psum((lax.psum_scatter(rhs_part, 'leg', scatter_dimension=0, tiled=Tr...  126 us
    reduce_scatter x1, waiting for transfers between devices, per_device(): lax.psum_scatter(block_part, 'leg', scatter_dimension=0, tiled=True)  71 us
    psum x1, blocking collectives, per_device(): lax.psum((jnp.sum(valid * primal * slack), jnp.sum(valid)), ('col', 'leg'))  66 us
    all_gather x4, blocking collectives, widen_all(): return lax.all_gather(vector, 'leg', axis=0, tiled=True)  48.6 us
    psum x5, blocking collectives, inner_sum(): return lax.psum(jnp.sum(left * right), 'leg')  47.1 us
  transfers between devices with their start and end apart: 6, of which 5 were waited for; matrix products, arithmetic and copies ran while one was open for 0% of the time, Pallas kernels for 0%

commit v1 on v0

--- a/solution.py
+++ b/solution.py
@@ -96,7 +96,11 @@
             scatter_dimension=0,
             tiled=True,
         )
-        image = lax.psum(narrow_shares, "col") + REGULAR * direction
+
+        def end_layers_all(v0, axis_id):
+            return jnp.sum(lax.all_gather(v0, axis_id), axis=0)
+
+        image = end_layers_all(narrow_shares, axis_id="col") + REGULAR * direction
         step_len = norm_now / inner_sum(direction, image)
         step_dual = step_dual + step_len * direction
         residual = residual - step_len * image

time: 1650 us -> 1350 us (0.82)
  blocking collectives: 679 us -> 375 us
    psum x3 -> x0, blocking collectives: 378 us -> none  [per_device(): image = lax.psum(narrow_shares, 'col') + REGULAR * direction]
    all_gather x0 -> x3, blocking collectives: none -> 74.8 us  [end_layers_all(): return jnp.sum(lax.all_gather(v0, axis_id), axis=0)]
  transfers between devices with their start and end apart: 6 -> 6, of which waited for: 5 -> 5; matrix products, arithmetic and copies ran while one was open for 0% -> 1% of each run, Pallas kernels for 0% -> 0%
where the time goes in v1:
time: 1350 us; the launch traced here: 1340 us
  other arithmetic  706 us (52%)
  blocking collectives  375 us (28%)
  waiting for transfers between devices  145 us (11%)
  matrix products  77.1 us (6%)
  between operations  23 us (2%)
  local copies, waits for them, and re-layouts  15.2 us (1%)
    another operation x4, other arithmetic, invert_one(): factor = jnp.linalg.cholesky(matrix)  376 us
    another operation x3, other arithmetic, invert_one(): return jax.scipy.linalg.cho_solve((factor, True), identity)  317 us
    psum x1, blocking collectives, per_device(): lax.psum((lax.psum_scatter(rhs_part, 'leg', scatter_dimension=0, tiled=Tr...  126 us
    all_gather x3, blocking collectives, end_layers_all(): return jnp.sum(lax.all_gather(v0, axis_id), axis=0)  74.8 us
    reduce_scatter x1, waiting for transfers between devices, per_device(): lax.psum_scatter(block_part, 'leg', scatter_dimension=0, tiled=True)  71 us
    psum x1, blocking collectives, per_device(): lax.psum((jnp.sum(valid * primal * slack), jnp.sum(valid)), ('col', 'leg'))  66 us
    reduce_scatter x3, waiting for transfers between devices, per_device(): lax.psum_scatter(forward_partial(scaling * transpose_apply(operate_whole)...  51.4 us
    all_gather x4, blocking collectives, widen_all(): return lax.all_gather(vector, 'leg', axis=0, tiled=True)  48.4 us
  transfers between devices with their start and end apart: 6, of which 5 were waited for; matrix products, arithmetic and copies ran while one was open for 1% of the time, Pallas kernels for 0%

profile of v1, /device:TPU:0, one launch (start us, length us, event | category | flops | bytes accessed | tf_op | source)
XLA Modules:
  0.0 1340.9 jit_solution(6864509317757547336)
XLA Ops:
  7.2 0.8 copy.20
  8.1 12.7 all_gather.33
  20.8 0.7 fusion.42
  21.5 0.2 fusion.28
  21.7 1.4 fusion.43
  23.1 66.0 %all-reduce = (f32[]{:T(128)}, f32[]{:T(128)}) all-reduce(f32[]{:T(128)} %get-tuple-element.5, f32[]{:T(128)} %get-tuple-element.4), channel_id=1, replica_groups=mesh['col'=32,'leg'=4] {'col','leg'}, use_global_device_ids=true, to_apply=%region_1.0 | all-reduce | flops 2 | bytes 16 | tf_op jit(solution)/shard_map/psum | solution.py:35
  90.5 4.3 fusion.18
  94.9 8.9 fusion
  103.8 9.6 fusion.2
  113.3 9.3 copy.22
  122.8 5.9 fusion.17
  128.6 1.0 convolution_negate_fusion
  129.7 71.0 %reduce-scatter.8.cloned.1.call-done = f32[32,128,128]{1,2,0:T(8,128)} async-done(((f32[128,128,128]{1,2,0:T(8,128)}), f32[32,128,128]{1,2,0:T(8,128)}) %reduce-scatter.8.cloned.1.call-update) | async-done | bytes 2097168 | tf_op jit(solution)/shard_map/reduce_scatter | solution.py:76
  200.9 22.2 %reduce-scatter.6.cloned.1.call-done = f32[32,128]{1,0:T(8,128)} async-done(((f32[128,128]{1,0:T(8,128)}), f32[32,128]{1,0:T(8,128)}) %reduce-scatter.6.cloned.1.call-update) | async-done | bytes 16400 | tf_op jit(solution)/shard_map/reduce_scatter | solution.py:75
  223.1 126.4 %psum.72 = f32[32,128]{1,0:T(8,128)S(1)} all-reduce(f32[32,128]{1,0:T(8,128)} %reduce-scatter.6.cloned.1.call-done), channel_id=1, replica_groups=mesh['col'=32,'leg'=4] {'col'}, use_global_device_ids=true, to_apply=%region_5.0 | all-reduce | flops 4096 | bytes 32768 | tf_op jit(solution)/shard_map/psum | solution.py:73
  349.5 3.3 broadcast_add_fusion
  352.8 2.9 copy.24
  355.7 3.2 fusion.8
  358.9 375.8 %custom-call.11 = f32[32,128,128]{2,1,0:T(8,128)S(1)} custom-call(f32[32,128,128]{2,1,0:T(8,128)} %fusion.8), custom_call_target="Cholesky" | custom-call | tf_op jit(solution)/shard_map/vmap(jit(cholesky))/cholesky | solution.py:16
  734.7 0.2 select_reduce_fusion
  735.0 1.7 select_bitcast_fusion
  736.7 315.5 %custom-call.12 = f32[32,1,128,128]{2,3,1,0:T(8,128)S(1)} custom-call(f32[32,1,128,128]{3,2,1,0:T(8,128)} %select_bitcast_fusion), custom_call_target="InvertDiagBlocksLowerTriangular" | custom-call | tf_op jit(solution)/shard_map/vmap(jit(_cho_solve))/triangular_solve | solution.py:17
  1052.2 1.3 copy-done.5
  1053.5 3.5 fusion.6
  1057.0 4.0 fusion.4
  1061.0 3.3 fusion.44
  1064.4 12.0 all_gather.34
  1076.4 0.2 fusion.26
  1076.6 2.4 fusion.15
  1079.1 3.7 fusion.14
  1082.8 1.0 fusion.25
  1083.8 15.1 %reduce-scatter.10.cloned.1.call-done = f32[32,128]{1,0:T(8,128)} async-done(((f32[128,128]{1,0:T(8,128)}), f32[32,128]{1,0:T(8,128)}) %reduce-scatter.10.cloned.1.call-update) | async-done | bytes 16400 | tf_op jit(solution)/shard_map/reduce_scatter | solution.py:93
  1099.0 24.9 %all-gather = f32[1024,128]{1,0:T(8,128)S(1)} all-gather(f32[32,128]{1,0:T(8,128)} %reduce-scatter.10.cloned.1.call-done), channel_id=2, replica_groups=mesh['col'=32,'leg'=4] {'col'}, dimensions={0}, use_global_device_ids=true | all-gather | bytes 540672 | tf_op jit(solution)/shard_map/all_gather | solution.py:101
  1124.0 0.6 multiply_reduce_fusion.3
  1124.6 9.2 all-reduce.1
  1135.1 3.3 fusion.45
  1138.4 0.6 multiply_reduce_fusion.2
  1139.0 9.5 psum.76
  1149.9 12.2 all_gather.37
  1162.1 0.2 fusion.24
  1162.4 4.2 fusion.13
  1166.6 3.7 fusion.12
  1170.3 1.0 fusion.23
  1171.3 18.1 %reduce-scatter.12.cloned.1.call-done = f32[32,128]{1,0:T(8,128)} async-done(((f32[128,128]{1,0:T(8,128)}), f32[32,128]{1,0:T(8,128)}) %reduce-scatter.12.cloned.1.call-update) | async-done | bytes 16400 | tf_op jit(solution)/shard_map/reduce_scatter | solution.py:93
  1189.4 25.0 %all-gather.1 = f32[1024,128]{1,0:T(8,128)S(1)} all-gather(f32[32,128]{1,0:T(8,128)} %reduce-scatter.12.cloned.1.call-done), channel_id=3, replica_groups=mesh['col'=32,'leg'=4] {'col'}, dimensions={0}, use_global_device_ids=true | all-gather | bytes 540672 | tf_op jit(solution)/shard_map/all_gather | solution.py:101
  1214.4 0.6 multiply_reduce_fusion.1
  1215.0 9.2 psum.77
  1225.5 3.3 fusion.46
  1228.9 0.6 multiply_reduce_fusion
  1229.5 9.5 psum.78
  1240.4 12.2 all_gather.40
  1252.6 0.2 fusion.22
  1252.8 4.2 fusion.11
  1257.0 3.7 fusion.10
  1260.8 1.0 fusion.21
  1261.7 18.1 %reduce-scatter.14.cloned.1.call-done = f32[32,128]{1,0:T(8,128)} async-done(((f32[128,128]{1,0:T(8,128)}), f32[32,128]{1,0:T(8,128)}) %reduce-scatter.14.cloned.1.call-update) | async-done | bytes 16400 | tf_op jit(solution)/shard_map/reduce_scatter | solution.py:93
  1279.9 24.9 %all-gather.2 = f32[1024,128]{1,0:T(8,128)S(1)} all-gather(f32[32,128]{1,0:T(8,128)} %reduce-scatter.14.cloned.1.call-done), channel_id=4, replica_groups=mesh['col'=32,'leg'=4] {'col'}, dimensions={0}, use_global_device_ids=true | all-gather | bytes 540672 | tf_op jit(solution)/shard_map/all_gather | solution.py:101
  1304.9 0.6 fusion.31
  1305.5 9.2 psum.79
  1316.0 11.9 all_gather.43
  1327.9 0.2 fusion.20
  1328.1 4.2 fusion.16
  1332.3 0.7 subtract_select_fusion
  1333.0 0.6 constant_dynamic-slice_fusion
  (53 shorter events, 1.0 us)
Async XLA Ops:
  7.2 87.7 %copy-start.6 = (f32[16,128]{1,0:T(8,128)S(1)}, f32[16,128]{1,0:T(8,128)}, u32[]{:S(2)}) copy-start(f32[16,128]{1,0:T(8,128)} %param.11) | copy-start | bytes 24580
  7.2 87.7 %copy-start.7 = (f32[16,128]{1,0:T(8,128)S(1)}, f32[16,128]{1,0:T(8,128)}, u32[]{:S(2)}) copy-start(f32[16,128]{1,0:T(8,128)} %param.12) | copy-start | bytes 24580
  7.2 87.7 %copy-start.8 = (f32[16,128]{1,0:T(8,128)S(1)}, f32[16,128]{1,0:T(8,128)}, u32[]{:S(2)}) copy-start(f32[16,128]{1,0:T(8,128)} %param.13) | copy-start | bytes 24580
  7.2 193.5 %reduce-scatter.8.cloned.1.call-start = ((), (), s32[]{:S(2)}) async-start(), calls=%async_computation.6 | async-start | bytes 10485760 | tf_op jit(solution)/shard_map/reduce_scatter | solution.py:76
  90.5 4.4 copy-start
  122.7 226.8 %copy-start.9 = (f32[32,128]{1,0:T(8,128)S(1)}, f32[32,128]{1,0:T(8,128)}, u32[]{:S(2)}) copy-start(f32[32,128]{1,0:T(8,128)} %param.15) | copy-start | bytes 49156
  122.7 100.3 %reduce-scatter.6.cloned.1.call-start = ((), (), s32[]{:S(2)}) async-start(), calls=%async_computation.5 | async-start | bytes 81920 | tf_op jit(solution)/shard_map/reduce_scatter | solution.py:75
  129.6 219.9 %all-reduce.4.cloned.1.call-start = ((), (), s32[]{:S(2)}) async-start(), calls=%async_computation.7 | async-start | bytes 4194304 | tf_op jit(solution)/shard_map/psum | solution.py:73
  200.7 898.3 %reduce-scatter.10.cloned.1.call-start = ((), (), s32[]{:S(2)}) async-start(), calls=%async_computation.8 | async-start | bytes 81920 | tf_op jit(solution)/shard_map/reduce_scatter | solution.py:93
  349.5 6.2 copy-start.4
  1052.2 1.4 copy-start.5
  1057.0 19.6 %copy-start.1 = (f32[16,4,128,128]{3,2,1,0:T(8,128)S(1)}, f32[16,4,128,128]{3,2,1,0:T(8,128)}, u32[]{:S(2)}) copy-start(f32[16,4,128,128]{3,2,1,0:T(8,128)} %param.8) | copy-start | bytes 12582916
  1083.8 105.6 %reduce-scatter.12.cloned.1.call-start = ((), (), s32[]{:S(2)}) async-start(), calls=%async_computation.9 | async-start | bytes 81920 | tf_op jit(solution)/shard_map/reduce_scatter | solution.py:93
  1149.9 16.6 %copy-start.2 = (f32[16,4,128,128]{3,2,1,0:T(8,128)S(1)}, f32[16,4,128,128]{3,2,1,0:T(8,128)}, u32[]{:S(2)}) copy-start(f32[16,4,128,128]{3,2,1,0:T(8,128)} %param.8) | copy-start | bytes 12582916
  1171.3 108.6 %reduce-scatter.14.cloned.1.call-start = ((), (), s32[]{:S(2)}) async-start(), calls=%async_computation.10 | async-start | bytes 81920 | tf_op jit(solution)/shard_map/reduce_scatter | solution.py:93
  1240.3 16.7 %copy-start.3 = (f32[16,4,128,128]{3,2,1,0:T(8,128)S(1)}, f32[16,4,128,128]{3,2,1,0:T(8,128)}, u32[]{:S(2)}) copy-start(f32[16,4,128,128]{3,2,1,0:T(8,128)} %param.8) | copy-start | bytes 12582916
  1257.0 75.3 %copy-start.10 = (s32[16]{0:T(128)S(1)}, s32[16]{0:T(128)}, u32[]{:S(2)}) copy-start(s32[16]{0:T(128)} %param.10) | copy-start | bytes 196
Sparse Core Ops, SparseCore 0:
  122.8 77.7 reduce-scatter.7
  203.0 20.0 reduce-scatter.5
  226.7 107.2 all-reduce.3
  1083.9 15.0 reduce-scatter.9
  1171.4 17.9 reduce-scatter.11
  1261.9 17.9 reduce-scatter.13
